TPU v7x, 32 devices: a whole 2x2x4 slice. The times are simulated.
32 devices in a mesh: expert: 2 (over y), seq: 16 (over z, x, core).
Axes of the slice: x: 2, y: 2, z: 4, core: 2. Of those that a mesh axis runs over, the one named last changes fastest.
Arguments:
- acts: bfloat16 [2, 2048, 1024], P('expert', 'seq'), may hold values from -6 to 6
- queries: bfloat16 [2, 2048, 1024], P('expert', 'seq'), may hold values from -32 to 32
- keys: bfloat16 [2, 2048, 1024], P('expert', 'seq'), may hold values from -6 to 6
- values: bfloat16 [2, 2048, 1024], P('expert', 'seq'), may hold values from -6 to 6
- grad_out: bfloat16 [2, 2048, 1024], P('expert', 'seq'), may hold values from -6 to 6
- gain: float32 [1024], replicated, may hold values from 0.5 to 1.5
- router: bfloat16 [1024, 2], replicated, may hold values from -0.1875 to 0.1875
- w_in: bfloat16 [2, 2048, 1024], P('expert', 'seq'), may hold values from -0.1875 to 0.1875
- w_out: bfloat16 [2, 2048, 1024], P('expert', 'seq'), may hold values from -0.125 to 0.125
- routes: int32 [2, 2048, 1], P('expert', 'seq'), may hold values from 0 to 1; in each aligned block of 128 rows (0 to 127, 128 to 255, ..., all dimensions but the last counted through in order) at most 80 rows name the same one
- tissue: int32 [2, 4], P('expert'), may hold values 0 or 1
Outputs:
- grad_acts: bfloat16 [2, 2048, 1024], P('expert', 'seq')
- grad_queries: bfloat16 [2, 2048, 1024], P('expert', 'seq')
- grad_keys: bfloat16 [2, 2048, 1024], P('expert', 'seq')
- grad_values: bfloat16 [2, 2048, 1024], P('expert', 'seq')
- grad_router: float32 [1024, 2], replicated
- grad_gain: float32 [1024], replicated
Inputs may be any that keep to these rules, and one draw needn't show every extreme that they name: `routes`: among the tiles of one run of 128 tiles of a slide, no expert is named more than 80 times, a bound that some block reaches.
All inputs are finite; a program needn't handle non-finite values. No bound on the sum of `tissue` on one device may be relied on, other than what follows from the above.
Results may differ from a plain program's by a relative error of at most 0.015.
Values may be sent and summed in bfloat16 or wider, within the bound.
A program may use at most 64 MiB of HBM per device.

v0:
```python
import functools

import jax
import jax.numpy as jnp
from jax import lax
from jax.experimental import pallas as pl
from jax.experimental.pallas import tpu as pltpu
from jax.sharding import PartitionSpec as P

HEAD = 64
REACH = 128
BLOCK = 512
EPS = 1e-06
LANES = 128
NEG = -1e30
GELU_C = 0.7978845608028654
GELU_A = 0.044715
MESH = pl.DeviceIdType.MESH


def dot(a, b, contract, precision=None):
    return lax.dot_general(
        a, b, (contract, ((), ())), preferred_element_type=jnp.float32, precision=precision
    )


def flip(index, mask):
    size = 1
    while size <= mask:
        if mask & size:
            index = index + size - 2 * size * ((index // size) % 2)
        size *= 2
    return index


def reduce_rounds(n, experts):
    bits = [(1 << b, 0) for b in range((experts - 1).bit_length())]
    bits += [(0, 1 << b) for b in range((n - 1).bit_length())]
    rounds = []
    for start in range(0, len(bits), 3):
        masks = [(0, 0)]
        for e, m in bits[start : start + 3]:
            masks += [(a + e, b + m) for a, b in masks]
        rounds.append(masks[1:])
    return rounds


def kernel(
    n, experts, cap, nblocks, groups,
    acts, queries, keys, values, grad_out, gain, router, w_in, w_out, routes, tissue,
    grad_acts, grad_q, grad_k, grad_v, small_out,
    weights, kx, vx, bias, probs, attn, normed_s, u_send, u_slots, g_send, g_slots,
    inner_acc, pick_acc, b_send, b_slots, p_send, p_slots, own_kv,
    low_send, high_send, low_recv, high_recv, red_send, red_recv,
    local_sem, halo_ss, halo_rs, w_ss, w_rs, ex_ss, ex_rs, rim_ss, rim_rs, red_ss, red_rs,
):
    tok, width = acts.shape
    span = tok + 2 * REACH
    frows = w_in.shape[0]
    rows = experts * cap
    pairs = width // LANES
    place = lax.axis_index("seq")
    me = lax.axis_index("expert")
    structured = n == 16
    bf16, f32 = jnp.bfloat16, jnp.float32

    def at(expert, seq):
        return (expert, seq)

    def remote(src, dst, ss, rs, where):
        return pltpu.make_async_remote_copy(
            src_ref=src, dst_ref=dst, send_sem=ss, recv_sem=rs, device_id=where, device_id_type=MESH
        )

    own_copies = [
        pltpu.make_async_copy(w_in, weights.at[place, 0], local_sem.at[0]),
        pltpu.make_async_copy(w_out, weights.at[place, 1], local_sem.at[1]),
        pltpu.make_async_copy(keys, kx.at[pl.ds(REACH, tok)], local_sem.at[2]),
        pltpu.make_async_copy(values, vx.at[pl.ds(REACH, tok)], local_sem.at[3]),
    ]
    for copy in own_copies:
        copy.start()

    barrier = pltpu.get_barrier_semaphore()
    rounds = reduce_rounds(n, experts)
    peers = [at(flip(me, e), flip(place, m)) for masks in rounds for e, m in masks]
    if structured:
        z = place // 4
        peers += [at(me, (place + 1) % n), at(me, (place + n - 1) % n)]
    else:
        peers += [at(me, (place + d) % n) for d in range(1, n)]
        peers += [at((me + d) % experts, place) for d in range(1, experts)]
    for peer in peers:
        pl.semaphore_signal(barrier, inc=1, device_id=peer, device_id_type=MESH)
    pl.semaphore_wait(barrier, len(peers))

    up, down = at(me, (place + 1) % n), at(me, (place + n - 1) % n)
    to_up = [
        remote(src, dst.at[pl.ds(0, REACH)], halo_ss.at[i, 0], halo_rs.at[i, 0], up)
        for i, (src, dst) in enumerate(((keys, kx), (values, vx)))
    ]
    to_down = [
        remote(src, dst.at[pl.ds(REACH + tok, REACH)], halo_ss.at[i, 1], halo_rs.at[i, 1], down)
        for i, (src, dst) in enumerate(((keys, kx), (values, vx)))
    ]

    @pl.when(place < n - 1)
    def _():
        for copy in to_up:
            copy.start()

    @pl.when(place > 0)
    def _():
        for copy in to_down:
            copy.start()

    own_copies[0].wait()
    own_copies[1].wait()

    def block(owner):
        return weights.at[owner]

    def push(owner, kind, step, where):
        return remote(block(owner), block(owner), w_ss.at[kind, step], w_rs.at[owner], where)

    def landed(owner):
        push(owner, 0, 0, up).wait_recv()

    if structured:
        x = (place // 2) % 2
        low = place % 4
        middle = (z == 1) | (z == 2)
        near, far = flip(place, 4), flip(place, 12)
        other_c = flip(place, 1)

        def column(k):
            return jnp.where(
                k == 0, z, jnp.where(k == 1, z + 1 - 2 * (z % 2), jnp.where(k == 2, 2 - z // 2, 3 - 3 * (z // 2)))
            )

        push(place, 0, 0, at(me, near)).start()

        @pl.when(middle)
        def _():
            push(place, 1, 0, at(me, far)).start()

        push(place, 2, 0, at(me, other_c)).start()
    else:

        def spread(d, carry):
            push(place, 0, d, at(me, (place + d) % n)).start()
            return carry

        lax.fori_loop(1, n, spread, 0)

    lane = lax.broadcasted_iota(jnp.int32, (tok, LANES), 1)
    row_at = lax.broadcasted_iota(jnp.int32, (tok, tok), 0)
    col_at = lax.broadcasted_iota(jnp.int32, (tok, tok), 1)
    spread_routes = jnp.where(row_at == col_at, jnp.broadcast_to(routes[...], (tok, tok)), 0)
    route = jnp.sum(spread_routes.astype(f32), -1, keepdims=True).astype(jnp.int32)
    onehot = (route == lane).astype(f32)
    lower = (row_at > col_at).astype(bf16)
    before = dot(lower, onehot.astype(bf16), ((1,), (0,)))
    rank = jnp.sum(before * onehot, -1, keepdims=True).astype(jnp.int32)
    slot = route * cap + rank
    disp = (slot == lax.broadcasted_iota(jnp.int32, (tok, rows), 1)).astype(bf16)

    here = x if structured else 0
    offsets = [(dx, d) for dx in range(groups) for d in range(experts)][1:]

    def beside(dx, d):
        return at((me + d) % experts, flip(place, 2 * dx))

    def exchange(piece, slots, which):
        return [
            remote(
                piece(here + dx * (1 - 2 * here), (me + d) % experts),
                slots.at[here, me],
                ex_ss.at[which, dx * experts + d],
                ex_rs.at[which, here * experts + me],
                beside(dx, d),
            )
            for dx, d in offsets
        ]

    def arrivals(slots, which):
        for dx, d in offsets:
            group, source = here + dx * (1 - 2 * here), (me + d) % experts
            remote(
                slots.at[group, source],
                slots.at[group, source],
                ex_ss.at[which, dx * experts + d],
                ex_rs.at[which, group * experts + source],
                beside(dx, d),
            ).wait_recv()

    moved_g = dot(disp, grad_out[...], ((0,), (0,))).astype(bf16)
    g_send[...] = moved_g.reshape(experts, cap, width)
    g_slots[here, me] = g_send[me]
    sends_g = exchange(lambda group, expert: g_send.at[expert], g_slots, 0)
    for copy in sends_g:
        copy.start()

    q_at = place * tok + lax.broadcasted_iota(jnp.int32, (tok, span), 0)
    k_at = place * tok - REACH + lax.broadcasted_iota(jnp.int32, (tok, span), 1)
    live = jnp.zeros((tok, span), jnp.int32)
    for b in range(nblocks):
        live = jnp.where((k_at >= b * BLOCK) & (k_at < (b + 1) * BLOCK), tissue[0, b], live)
    near_by = jnp.abs(q_at - k_at) <= REACH
    allow = near_by & (k_at >= 0) & (k_at < n * tok) & ((live == 1) | (q_at == k_at))
    bias[...] = jnp.where(allow, 0.0, NEG).astype(f32)
    half = lax.broadcasted_iota(jnp.int32, (tok, LANES), 1) < HEAD
    first = half.astype(bf16)
    second = (1.0 - half.astype(f32)).astype(bf16)

    def stack(value):
        return jnp.concatenate([value * first, value * second], 0)

    own_copies[2].wait()
    own_copies[3].wait()

    @pl.when(place > 0)
    def _():
        for copy in to_up:
            copy.wait_recv()

    @pl.when(place == 0)
    def _():
        kx[pl.ds(0, REACH), :] = jnp.zeros((REACH, width), bf16)
        vx[pl.ds(0, REACH), :] = jnp.zeros((REACH, width), bf16)

    @pl.when(place < n - 1)
    def _():
        for copy in to_down:
            copy.wait_recv()

    @pl.when(place == n - 1)
    def _():
        kx[pl.ds(REACH + tok, REACH), :] = jnp.zeros((REACH, width), bf16)
        vx[pl.ds(REACH + tok, REACH), :] = jnp.zeros((REACH, width), bf16)

    def forward(i, carry):
        cols = pl.ds(pl.multiple_of(i * LANES, LANES), LANES)
        scores = dot(stack(queries[:, cols]), kx[:, cols], ((1,), (1,))) * HEAD ** (-0.5)
        both = jnp.concatenate([bias[...], bias[...]], 0)
        scores = scores + both
        weight = jnp.exp(scores - jnp.max(scores, -1, keepdims=True))
        prob = weight / jnp.sum(weight, -1, keepdims=True)
        probs[i] = prob
        mixed = dot(prob.astype(bf16), vx[:, cols], ((1,), (0,)))
        attn[:, cols] = jnp.where(half, mixed[:tok], mixed[tok:])
        return carry

    lax.fori_loop(0, pairs, forward, 0)

    mid = acts[...].astype(f32) + attn[...]
    rms = lax.rsqrt(jnp.mean(mid * mid, -1, keepdims=True) + EPS)
    normed_s[...] = mid * rms
    inner = (normed_s[...] * gain[...]).astype(bf16)
    moved_u = dot(disp, inner, ((0,), (0,))).astype(bf16)
    u_send[...] = moved_u.reshape(experts, cap, width)
    u_slots[here, me] = u_send[me]
    sends_u = exchange(lambda group, expert: u_send.at[expert], u_slots, 1)
    for copy in sends_u:
        copy.start()

    inner_f = inner.astype(f32)
    router_f = router[...].astype(f32)
    r_lane = lane
    logits = jnp.full((tok, LANES), NEG, f32)
    for e in range(experts):
        logits = jnp.where(lane == e, jnp.sum(inner_f * router_f[e : e + 1, :], -1, keepdims=True), logits)
    chance = jnp.exp(logits - jnp.max(logits, -1, keepdims=True))
    chance = chance / jnp.sum(chance, -1, keepdims=True)
    chosen = (route == r_lane).astype(f32)
    pick = jnp.sum(chance * chosen, -1, keepdims=True)

    inner_acc[...] = jnp.zeros_like(inner_acc)
    pick_acc[...] = jnp.zeros_like(pick_acc)
    per = max(1, 256 // frows)

    def work(start):
        flat_u = u_slots[...].reshape(groups * rows, width)
        flat_g = g_slots[...].reshape(groups * rows, width)
        wi = weights[pl.ds(start, per), 0].reshape(per * frows, width)
        wo = weights[pl.ds(start, per), 1].reshape(per * frows, width)
        hidden = dot(flat_u, wi, ((1,), (1,)))
        back = dot(flat_g, wo, ((1,), (1,)))
        square = hidden * hidden
        t = jnp.tanh(GELU_C * hidden * (1.0 + GELU_A * square))
        gate = 0.5 * (1.0 + t)
        act = (hidden * gate).astype(bf16).astype(f32)
        slope = gate + 0.5 * hidden * (1.0 - t * t) * (GELU_C * (1.0 + 3.0 * GELU_A * square))
        pick_acc[...] += jnp.sum(act * back, -1, keepdims=True)
        inner_acc[...] += dot((back * slope).astype(bf16), wi, ((1,), (0,)))

    if structured:

        def relay(k):
            owner = column(k) * 4 + low

            @pl.when((k > 0) & (k < 4))
            def _():
                landed(owner)

                @pl.when(middle)
                def _():
                    push(owner, 0, k, at(me, jnp.where(k == 1, far, near))).start()

                push(owner, 2, k, at(me, other_c)).start()

        relay(1)
        relay(2)

        @pl.when(middle)
        def _():
            relay(3)

        arrivals(g_slots, 0)
        arrivals(u_slots, 1)

        def step(k, carry):
            start = column(k) * 4 + x * 2

            @pl.when((k == 2) & jnp.logical_not(middle))
            def _():
                relay(3)

            landed(start + 1 - place % 2)
            work(start)
            return carry

        lax.fori_loop(0, 4, step, 0)
    else:

        def settle(d, carry):
            landed((place + d) % n)
            return carry

        lax.fori_loop(1, n, settle, 0)
        arrivals(g_slots, 0)
        arrivals(u_slots, 1)

        def step(j, carry):
            work(j * per)
            return carry

        lax.fori_loop(0, n // per, step, 0)

    b_send[...] = inner_acc[...].astype(bf16).reshape(groups, experts, cap, width)
    p_send[...] = jnp.broadcast_to(pick_acc[...], (groups * rows, LANES)).reshape(groups, experts, cap, LANES)
    sends_b = exchange(lambda group, expert: b_send.at[group, expert], b_slots, 2)
    sends_p = exchange(lambda group, expert: p_send.at[group, expert], p_slots, 3)
    for copy in sends_p + sends_b:
        copy.start()
    b_slots[here, me] = b_send[here, me]
    p_slots[here, me] = p_send[here, me]
    arrivals(p_slots, 3)
    arrivals(b_slots, 2)

    normed = normed_s[...]
    part_inner = dot(disp, b_slots[0].reshape(rows, width), ((1,), (0,)))
    picks = p_slots[0].reshape(rows, LANES)
    for group in range(1, groups):
        part_inner = part_inner + dot(disp, b_slots[group].reshape(rows, width), ((1,), (0,)))
        picks = picks + p_slots[group].reshape(rows, LANES)
    grad_pick = dot(disp.astype(f32), picks, ((1,), (0,)), lax.Precision.HIGHEST)[:, :1]
    grad_logits = (grad_pick * pick) * (chosen - chance)
    grad_inner = pick * part_inner
    inner_f = (normed * gain[...]).astype(bf16).astype(f32)
    for e in range(experts):
        column_e = grad_logits[:, e : e + 1]
        grad_inner = grad_inner + column_e * router_f[e : e + 1, :]
        red_send[0, e : e + 1, :] = jnp.sum(inner_f * column_e, 0, keepdims=True)
    red_send[0, experts : experts + 1, :] = jnp.sum(grad_inner * normed, 0, keepdims=True)
    filler = red_send.shape[1] - experts - 1
    if filler:
        red_send[0, experts + 1 :, :] = jnp.zeros((filler, width), f32)
    grad_normed = grad_inner * gain[...]
    grad_mid = rms * (
        grad_normed - normed * jnp.mean(grad_normed * normed, -1, keepdims=True)
    ) + grad_out[...].astype(f32)
    grad_acts[...] = grad_mid.astype(bf16)

    reduces = [
        [
            remote(red_send.at[j], red_recv.at[j, i], red_ss.at[j, i], red_rs.at[j, i], at(flip(me, e), flip(place, m)))
            for i, (e, m) in enumerate(masks)
        ]
        for j, masks in enumerate(rounds)
    ]

    def reduce_step(j):
        total = red_send[j]
        for i, copy in enumerate(reduces[j]):
            copy.wait_recv()
            total = total + red_recv[j, i]
        if j + 1 < len(reduces):
            red_send[j + 1] = total
            for copy in reduces[j + 1]:
                copy.start()
        else:
            small_out[...] = total

    for copy in reduces[0]:
        copy.start()

    def rim_down(i):
        return remote(low_send.at[i], low_recv.at[i], rim_ss.at[0, i], rim_rs.at[0, i], down)

    def rim_up(i):
        return remote(high_send.at[i], high_recv.at[i], rim_ss.at[1, i], rim_rs.at[1, i], up)

    def backward(i, carry):
        for j in range(len(reduces) - 1):

            @pl.when(i == 4 + j)
            def _():
                reduce_step(j)

        cols = pl.ds(pl.multiple_of(i * LANES, LANES), LANES)
        o_stack = stack(grad_acts[:, cols])
        q_stack = stack(queries[:, cols])
        prob = probs[i]
        grad_probs = dot(o_stack, vx[:, cols], ((1,), (1,)))
        value_terms = dot(prob.astype(bf16), o_stack, ((0,), (0,)))
        delta = jnp.sum(prob * grad_probs, -1, keepdims=True)
        grad_scores = (prob * (grad_probs - delta) * HEAD ** (-0.5)).astype(bf16)
        query_terms = dot(grad_scores, kx[:, cols], ((1,), (0,)))
        grad_q[:, cols] = jnp.where(half, query_terms[:tok], query_terms[tok:]).astype(bf16)
        key_terms = dot(grad_scores, q_stack, ((0,), (0,)))
        for slot_at, terms in enumerate((key_terms, value_terms)):
            low_send[i, slot_at] = terms[:REACH].astype(bf16)
            own_kv[slot_at, :, cols] = terms[REACH : REACH + tok]
            high_send[i, slot_at] = terms[REACH + tok :].astype(bf16)

        @pl.when(place > 0)
        def _():
            rim_down(i).start()

        @pl.when(place < n - 1)
        def _():
            rim_up(i).start()

        return carry

    lax.fori_loop(0, pairs, backward, 0)
    reduce_step(len(reduces) - 1)

    def finish(i, carry):
        cols = pl.ds(pl.multiple_of(i * LANES, LANES), LANES)

        @pl.when(place > 0)
        def _():
            rim_up(i).wait_recv()
            for slot_at in range(2):
                own_kv[slot_at, :REACH, cols] += high_recv[i, slot_at].astype(f32)

        @pl.when(place < n - 1)
        def _():
            rim_down(i).wait_recv()
            for slot_at in range(2):
                own_kv[slot_at, tok - REACH :, cols] += low_recv[i, slot_at].astype(f32)

        grad_k[:, cols] = own_kv[0, :, cols].astype(bf16)
        grad_v[:, cols] = own_kv[1, :, cols].astype(bf16)
        return carry

    lax.fori_loop(0, pairs, finish, 0)

    @pl.when(place < n - 1)
    def _():
        for copy in to_up:
            copy.wait_send()

    @pl.when(place > 0)
    def _():
        for copy in to_down:
            copy.wait_send()

    for copy in sends_g + sends_u + sends_b + sends_p + [c for group in reduces for c in group]:
        copy.wait_send()

    def drain(i, carry):
        @pl.when(place > 0)
        def _():
            rim_down(i).wait_send()

        @pl.when(place < n - 1)
        def _():
            rim_up(i).wait_send()

        return carry

    lax.fori_loop(0, pairs, drain, 0)
    if structured:
        push(place, 0, 0, at(me, near)).wait_send()

        @pl.when(middle)
        def _():
            push(place, 1, 0, at(me, far)).wait_send()

        def sent(k, carry):
            @pl.when((k > 0) & middle)
            def _():
                push(place, 0, k, at(me, near)).wait_send()

            push(place, 2, k, at(me, near)).wait_send()
            return carry

        lax.fori_loop(0, 4, sent, 0)
    else:

        def sent(d, carry):
            push(place, 0, d, at(me, (place + d) % n)).wait_send()
            return carry

        lax.fori_loop(1, n, sent, 0)


def shards(acts, queries, keys, values, grad_out, gain, router, w_in, w_out, routes, tissue):
    tok, width = acts.shape[1:]
    n = lax.axis_size("seq")
    experts = router.shape[1]
    cap = max(2, 5 * tok // (4 * experts))
    cap = -(-cap // 16) * 16
    rows = experts * cap
    frows = w_in.shape[1]
    span = tok + 2 * REACH
    pairs = width // LANES
    lines = -(-(experts + 1) // 8) * 8
    rounds = reduce_rounds(n, experts)
    most = max(len(masks) for masks in rounds)
    groups = 2 if n == 16 else 1
    bf16, f32 = jnp.bfloat16, jnp.float32
    vmem = pl.BlockSpec(memory_space=pltpu.VMEM)
    big = jax.ShapeDtypeStruct((tok, width), bf16)
    dma = pltpu.SemaphoreType.DMA
    steps = 4 if n == 16 else n
    outs = pl.pallas_call(
        functools.partial(kernel, n, experts, cap, tissue.shape[1], groups),
        out_shape=[big, big, big, big, jax.ShapeDtypeStruct((lines, width), f32)],
        in_specs=[vmem] * 10 + [pl.BlockSpec(memory_space=pltpu.SMEM)],
        out_specs=[vmem] * 5,
        scratch_shapes=[
            pltpu.VMEM((n, 2, frows, width), bf16),
            pltpu.VMEM((span, width), bf16),
            pltpu.VMEM((span, width), bf16),
            pltpu.VMEM((tok, span), f32),
            pltpu.VMEM((pairs, 2 * tok, span), f32),
            pltpu.VMEM((tok, width), f32),
            pltpu.VMEM((tok, width), f32),
            pltpu.VMEM((experts, cap, width), bf16),
            pltpu.VMEM((groups, experts, cap, width), bf16),
            pltpu.VMEM((experts, cap, width), bf16),
            pltpu.VMEM((groups, experts, cap, width), bf16),
            pltpu.VMEM((groups * rows, width), f32),
            pltpu.VMEM((groups * rows, 1), f32),
            pltpu.VMEM((groups, experts, cap, width), bf16),
            pltpu.VMEM((groups, experts, cap, width), bf16),
            pltpu.VMEM((groups, experts, cap, LANES), f32),
            pltpu.VMEM((groups, experts, cap, LANES), f32),
            pltpu.VMEM((2, tok, width), f32),
            pltpu.VMEM((pairs, 2, REACH, LANES), bf16),
            pltpu.VMEM((pairs, 2, REACH, LANES), bf16),
            pltpu.VMEM((pairs, 2, REACH, LANES), bf16),
            pltpu.VMEM((pairs, 2, REACH, LANES), bf16),
            pltpu.VMEM((len(rounds), lines, width), f32),
            pltpu.VMEM((len(rounds), most, lines, width), f32),
            dma((4,)),
            dma((2, 2)),
            dma((2, 2)),
            dma((3, steps)),
            dma((n,)),
            dma((4, groups * experts)),
            dma((4, groups * experts)),
            dma((2, pairs)),
            dma((2, pairs)),
            dma((len(rounds), most)),
            dma((len(rounds), most)),
        ],
        compiler_params=pltpu.CompilerParams(
            collective_id=0, has_side_effects=True, vmem_limit_bytes=60 * 1024 * 1024
        ),
    )(
        acts[0], queries[0], keys[0], values[0], grad_out[0], gain[None], router.T,
        w_in[0], w_out[0], routes[:, :, 0], tissue,
    )
    outs = pl.pallas_call(
        hand_out,
        out_shape=[
            big, big, big, big,
            jax.ShapeDtypeStruct((experts, width), f32), jax.ShapeDtypeStruct((1, width), f32),
        ],
        in_specs=[vmem] * 5,
        out_specs=[vmem] * 6,
    )(*outs)
    return tuple(out[None] for out in outs[:4]) + (outs[4].T, outs[5][0])


def hand_out(*refs):
    for source, target in zip(refs[:4], refs[5:9]):
        target[...] = source[...]
    experts = refs[9].shape[0]
    refs[9][...] = refs[4][:experts, :]
    refs[10][...] = refs[4][experts : experts + 1, :]


def solution(mesh):
    tiles = P("expert", "seq", None)
    in_specs = (tiles,) * 5 + (P(), P()) + (tiles,) * 3 + (P("expert", None),)
    out_specs = (tiles,) * 4 + (P(), P())
    return jax.shard_map(shards, mesh=mesh, in_specs=in_specs, out_specs=out_specs, check_vma=False)
```

profile of v0, /device:TPU:1, one launch (start us, length us, event | category | flops | bytes accessed | tf_op | source)
XLA Modules:
  0.0 85.6 jit_solution(11559486705477073250)
XLA Ops:
  0.6 82.8 %shard_map.154 = (bf16[128,1024]{1,0:T(8,128)(2,1)}, bf16[128,1024]{1,0:T(8,128)(2,1)}, bf16[128,1024]{1,0:T(8,128)(2,1)}, bf16[128,1024]{1,0:T(8,128)(2,1)}, f32[8,1024]{1,0:T(8,128)}) custom-call(bf16[128,1024]{1,0:T(8,128)(2,1)} %bitcast.16, bf16[128,1024]{1,0:T(8,128)(2,1)} %bitcast.17, bf16[128,1024]{1,0:T(8,128)(2,1)} %bitcast.18, ...), custom_call_target="tpu_custom_call" | custom-call | tf_op jit(solution)/shard_map/pallas_call | solution.py:540
  83.5 2.2 %shard_map.155 = (bf16[128,1024]{1,0:T(8,128)(2,1)}, bf16[128,1024]{1,0:T(8,128)(2,1)}, bf16[128,1024]{1,0:T(8,128)(2,1)}, bf16[128,1024]{1,0:T(8,128)(2,1)}, f32[2,1024]{1,0:T(2,128)}, /*index=5*/f32[1,1024]{1,0:T(1,128)}) custom-call(bf16[128,1024]{1,0:T(8,128)(2,1)} %get-tuple-element.17.refs_0_, bf16[128,1024]{1,0:T(8,128)(2,1)} %get-tuple-element.18.refs_1_, ...), custom_call_target="tpu_custom_call" | custom-call | tf_op jit(solution)/shard_map/pallas_call | solution.py:589
where the time goes:
time: 86 us; the launch traced here: 85.6 us
  Pallas kernels  85 us (99%)
    pallas_call x1, Pallas kernels, shards(): pl.pallas_call(functools.partial(kernel, n, experts, cap, tissue.shape[1]...  82.8 us
    pallas_call x1, Pallas kernels, shards(): pl.pallas_call(hand_out, out_shape=[big, big, big, big, jax.ShapeDtypeStr...  2.18 us

commit v1 on v0

--- a/solution.py
+++ b/solution.py
@@ -47,14 +47,15 @@
 
 def kernel(
     n, experts, cap, nblocks, groups,
-    acts, queries, keys, values, grad_out, gain, router, w_in, w_out, routes, tissue,
-    grad_acts, grad_q, grad_k, grad_v, small_out,
+    acts_h, queries_h, keys, values, grad_out_h, gain, router, w_in, w_out, routes, tissue,
+    grad_acts_h, grad_q_h, grad_k_h, grad_v_h, small_out,
+    acts, queries, grad_out, grad_acts, grad_q, grad_k, grad_v, act_s, slope_s,
     weights, kx, vx, bias, probs, attn, normed_s, u_send, u_slots, g_send, g_slots,
     inner_acc, pick_acc, b_send, b_slots, p_send, p_slots, own_kv,
     low_send, high_send, low_recv, high_recv, red_send, red_recv,
-    local_sem, halo_ss, halo_rs, w_ss, w_rs, ex_ss, ex_rs, rim_ss, rim_rs, red_ss, red_rs,
+    local_sem, out_sem, halo_ss, halo_rs, w_ss, w_rs, ex_ss, ex_rs, rim_ss, rim_rs, red_ss, red_rs,
 ):
-    tok, width = acts.shape
+    tok, width = acts_h.shape
     span = tok + 2 * REACH
     frows = w_in.shape[0]
     rows = experts * cap
@@ -71,15 +72,6 @@
         return pltpu.make_async_remote_copy(
             src_ref=src, dst_ref=dst, send_sem=ss, recv_sem=rs, device_id=where, device_id_type=MESH
         )
-
-    own_copies = [
-        pltpu.make_async_copy(w_in, weights.at[place, 0], local_sem.at[0]),
-        pltpu.make_async_copy(w_out, weights.at[place, 1], local_sem.at[1]),
-        pltpu.make_async_copy(keys, kx.at[pl.ds(REACH, tok)], local_sem.at[2]),
-        pltpu.make_async_copy(values, vx.at[pl.ds(REACH, tok)], local_sem.at[3]),
-    ]
-    for copy in own_copies:
-        copy.start()
 
     barrier = pltpu.get_barrier_semaphore()
     rounds = reduce_rounds(n, experts)
@@ -92,67 +84,18 @@
         peers += [at((me + d) % experts, place) for d in range(1, experts)]
     for peer in peers:
         pl.semaphore_signal(barrier, inc=1, device_id=peer, device_id_type=MESH)
-    pl.semaphore_wait(barrier, len(peers))
-
-    up, down = at(me, (place + 1) % n), at(me, (place + n - 1) % n)
-    to_up = [
-        remote(src, dst.at[pl.ds(0, REACH)], halo_ss.at[i, 0], halo_rs.at[i, 0], up)
-        for i, (src, dst) in enumerate(((keys, kx), (values, vx)))
+
+    own_copies = [
+        pltpu.make_async_copy(w_in, weights.at[place, 0], local_sem.at[0]),
+        pltpu.make_async_copy(w_out, weights.at[place, 1], local_sem.at[1]),
+        pltpu.make_async_copy(keys, kx.at[pl.ds(REACH, tok)], local_sem.at[2]),
+        pltpu.make_async_copy(values, vx.at[pl.ds(REACH, tok)], local_sem.at[3]),
+        pltpu.make_async_copy(grad_out_h, grad_out, local_sem.at[4]),
+        pltpu.make_async_copy(queries_h, queries, local_sem.at[5]),
+        pltpu.make_async_copy(acts_h, acts, local_sem.at[6]),
     ]
-    to_down = [
-        remote(src, dst.at[pl.ds(REACH + tok, REACH)], halo_ss.at[i, 1], halo_rs.at[i, 1], down)
-        for i, (src, dst) in enumerate(((keys, kx), (values, vx)))
-    ]
-
-    @pl.when(place < n - 1)
-    def _():
-        for copy in to_up:
-            copy.start()
-
-    @pl.when(place > 0)
-    def _():
-        for copy in to_down:
-            copy.start()
-
-    own_copies[0].wait()
-    own_copies[1].wait()
-
-    def block(owner):
-        return weights.at[owner]
-
-    def push(owner, kind, step, where):
-        return remote(block(owner), block(owner), w_ss.at[kind, step], w_rs.at[owner], where)
-
-    def landed(owner):
-        push(owner, 0, 0, up).wait_recv()
-
-    if structured:
-        x = (place // 2) % 2
-        low = place % 4
-        middle = (z == 1) | (z == 2)
-        near, far = flip(place, 4), flip(place, 12)
-        other_c = flip(place, 1)
-
-        def column(k):
-            return jnp.where(
-                k == 0, z, jnp.where(k == 1, z + 1 - 2 * (z % 2), jnp.where(k == 2, 2 - z // 2, 3 - 3 * (z // 2)))
-            )
-
-        push(place, 0, 0, at(me, near)).start()
-
-        @pl.when(middle)
-        def _():
-            push(place, 1, 0, at(me, far)).start()
-
-        push(place, 2, 0, at(me, other_c)).start()
-    else:
-
-        def spread(d, carry):
-            push(place, 0, d, at(me, (place + d) % n)).start()
-            return carry
-
-        lax.fori_loop(1, n, spread, 0)
-
+    for copy in own_copies:
+        copy.start()
     lane = lax.broadcasted_iota(jnp.int32, (tok, LANES), 1)
     row_at = lax.broadcasted_iota(jnp.int32, (tok, tok), 0)
     col_at = lax.broadcasted_iota(jnp.int32, (tok, tok), 1)
@@ -165,7 +108,85 @@
     slot = route * cap + rank
     disp = (slot == lax.broadcasted_iota(jnp.int32, (tok, rows), 1)).astype(bf16)
 
-    here = x if structured else 0
+    here = (place // 2) % 2 if structured else 0
+    q_at = place * tok + lax.broadcasted_iota(jnp.int32, (tok, span), 0)
+    k_at = place * tok - REACH + lax.broadcasted_iota(jnp.int32, (tok, span), 1)
+    live = jnp.zeros((tok, span), jnp.int32)
+    for b in range(nblocks):
+        live = jnp.where((k_at >= b * BLOCK) & (k_at < (b + 1) * BLOCK), tissue[0, b], live)
+    near_by = jnp.abs(q_at - k_at) <= REACH
+    allow = near_by & (k_at >= 0) & (k_at < n * tok) & ((live == 1) | (q_at == k_at))
+    bias[...] = jnp.where(allow, 0.0, NEG).astype(f32)
+    own_copies[4].wait()
+    moved_g = dot(disp, grad_out[...], ((0,), (0,))).astype(bf16)
+    g_send[...] = moved_g.reshape(experts, cap, width)
+    g_slots[here, me] = g_send[me]
+    pl.semaphore_wait(barrier, len(peers))
+
+    up, down = at(me, (place + 1) % n), at(me, (place + n - 1) % n)
+    to_up = [
+        remote(src, dst.at[pl.ds(0, REACH)], halo_ss.at[i, 0], halo_rs.at[i, 0], up)
+        for i, (src, dst) in enumerate(((keys, kx), (values, vx)))
+    ]
+    to_down = [
+        remote(src, dst.at[pl.ds(REACH + tok, REACH)], halo_ss.at[i, 1], halo_rs.at[i, 1], down)
+        for i, (src, dst) in enumerate(((keys, kx), (values, vx)))
+    ]
+
+    @pl.when(place < n - 1)
+    def _():
+        for copy in to_up:
+            copy.start()
+
+    @pl.when(place > 0)
+    def _():
+        for copy in to_down:
+            copy.start()
+
+    def push(owner, j, kind, step, where, src=None):
+        return remote(
+            weights.at[owner, j] if src is None else src,
+            weights.at[owner, j],
+            w_ss.at[kind, step, j],
+            w_rs.at[owner, j],
+            where,
+        )
+
+    def landed(owner, j):
+        push(owner, j, 0, 0, up).wait_recv()
+
+    mine = (w_in, w_out)
+    if structured:
+        x = (place // 2) % 2
+        low = place % 4
+        middle = (z == 1) | (z == 2)
+        near, far = flip(place, 4), flip(place, 12)
+        other_c = flip(place, 1)
+
+        def column(k):
+            return jnp.where(
+                k == 0, z, jnp.where(k == 1, z + 1 - 2 * (z % 2), jnp.where(k == 2, 2 - z // 2, 3 - 3 * (z // 2)))
+            )
+
+        for j in range(2):
+            push(place, j, 0, 0, at(me, near), mine[j]).start()
+
+        @pl.when(middle)
+        def _():
+            for j in range(2):
+                push(place, j, 1, 0, at(me, far), mine[j]).start()
+
+        for j in range(2):
+            push(place, j, 2, 0, at(me, other_c), mine[j]).start()
+    else:
+
+        def spread(d, carry):
+            for j in range(2):
+                push(place, j, 0, d, at(me, (place + d) % n), mine[j]).start()
+            return carry
+
+        lax.fori_loop(1, n, spread, 0)
+
     offsets = [(dx, d) for dx in range(groups) for d in range(experts)][1:]
 
     def beside(dx, d):
@@ -194,21 +215,6 @@
                 beside(dx, d),
             ).wait_recv()
 
-    moved_g = dot(disp, grad_out[...], ((0,), (0,))).astype(bf16)
-    g_send[...] = moved_g.reshape(experts, cap, width)
-    g_slots[here, me] = g_send[me]
-    sends_g = exchange(lambda group, expert: g_send.at[expert], g_slots, 0)
-    for copy in sends_g:
-        copy.start()
-
-    q_at = place * tok + lax.broadcasted_iota(jnp.int32, (tok, span), 0)
-    k_at = place * tok - REACH + lax.broadcasted_iota(jnp.int32, (tok, span), 1)
-    live = jnp.zeros((tok, span), jnp.int32)
-    for b in range(nblocks):
-        live = jnp.where((k_at >= b * BLOCK) & (k_at < (b + 1) * BLOCK), tissue[0, b], live)
-    near_by = jnp.abs(q_at - k_at) <= REACH
-    allow = near_by & (k_at >= 0) & (k_at < n * tok) & ((live == 1) | (q_at == k_at))
-    bias[...] = jnp.where(allow, 0.0, NEG).astype(f32)
     half = lax.broadcasted_iota(jnp.int32, (tok, LANES), 1) < HEAD
     first = half.astype(bf16)
     second = (1.0 - half.astype(f32)).astype(bf16)
@@ -238,6 +244,30 @@
     def _():
         kx[pl.ds(REACH + tok, REACH), :] = jnp.zeros((REACH, width), bf16)
         vx[pl.ds(REACH + tok, REACH), :] = jnp.zeros((REACH, width), bf16)
+
+    sends_g = exchange(lambda group, expert: g_send.at[expert], g_slots, 0)
+    for copy in sends_g:
+        copy.start()
+    own_copies[5].wait()
+
+    if structured:
+
+        def relay(k):
+            owner = column(k) * 4 + low
+            for j in range(2):
+                landed(owner, j)
+
+                @pl.when(middle)
+                def _():
+                    push(owner, j, 0, k, at(me, jnp.where(k == 1, far, near))).start()
+
+                push(owner, j, 2, k, at(me, other_c)).start()
+
+        relay(1)
+
+        @pl.when(middle)
+        def _():
+            relay(2)
 
     def forward(i, carry):
         cols = pl.ds(pl.multiple_of(i * LANES, LANES), LANES)
@@ -253,6 +283,7 @@
 
     lax.fori_loop(0, pairs, forward, 0)
 
+    own_copies[6].wait()
     mid = acts[...].astype(f32) + attn[...]
     rms = lax.rsqrt(jnp.mean(mid * mid, -1, keepdims=True) + EPS)
     normed_s[...] = mid * rms
@@ -275,66 +306,94 @@
     chosen = (route == r_lane).astype(f32)
     pick = jnp.sum(chance * chosen, -1, keepdims=True)
 
+    own_copies[0].wait()
+    own_copies[1].wait()
     inner_acc[...] = jnp.zeros_like(inner_acc)
     pick_acc[...] = jnp.zeros_like(pick_acc)
     per = max(1, 256 // frows)
 
-    def work(start):
-        flat_u = u_slots[...].reshape(groups * rows, width)
-        flat_g = g_slots[...].reshape(groups * rows, width)
-        wi = weights[pl.ds(start, per), 0].reshape(per * frows, width)
-        wo = weights[pl.ds(start, per), 1].reshape(per * frows, width)
-        hidden = dot(flat_u, wi, ((1,), (1,)))
-        back = dot(flat_g, wo, ((1,), (1,)))
+    span_w = per * frows
+
+    def first_half(start):
+        wi = weights[pl.ds(start, per), 0].reshape(span_w, width)
+        hidden = dot(u_slots[...].reshape(groups * rows, width), wi, ((1,), (1,)))
         square = hidden * hidden
         t = jnp.tanh(GELU_C * hidden * (1.0 + GELU_A * square))
         gate = 0.5 * (1.0 + t)
         act = (hidden * gate).astype(bf16).astype(f32)
         slope = gate + 0.5 * hidden * (1.0 - t * t) * (GELU_C * (1.0 + 3.0 * GELU_A * square))
-        pick_acc[...] += jnp.sum(act * back, -1, keepdims=True)
-        inner_acc[...] += dot((back * slope).astype(bf16), wi, ((1,), (0,)))
+        act_s[...] = act.reshape(groups, rows, span_w)
+        slope_s[...] = slope.reshape(groups, rows, span_w)
+
+    def second_half(start):
+        wi = weights[pl.ds(start, per), 0].reshape(span_w, width)
+        wo = weights[pl.ds(start, per), 1].reshape(span_w, width)
+        back = dot(g_slots[...].reshape(groups * rows, width), wo, ((1,), (1,)))
+        act = act_s[...].reshape(groups * rows, span_w)
+        slope = slope_s[...].reshape(groups * rows, span_w)
+        pick_acc[...] += jnp.sum(act * back, -1, keepdims=True).reshape(groups, rows, 1)
+        inner_acc[...] += dot((back * slope).astype(bf16), wi, ((1,), (0,))).reshape(groups, rows, width)
+
+    eye = (
+        lax.broadcasted_iota(jnp.int32, (cap, LANES), 0) == lax.broadcasted_iota(jnp.int32, (cap, LANES), 1)
+    ).astype(f32)
+
+    def last_half(start, group):
+        wi = weights[pl.ds(start, per), 0].reshape(span_w, width)
+        wo = weights[pl.ds(start, per), 1].reshape(span_w, width)
+        back = dot(g_slots[group].reshape(rows, width), wo, ((1,), (1,)))
+        picked = pick_acc[group] + jnp.sum(act_s[group] * back, -1, keepdims=True)
+        total = inner_acc[group] + dot((back * slope_s[group]).astype(bf16), wi, ((1,), (0,)))
+        b_send[group] = total.astype(bf16).reshape(experts, cap, width)
+        for e in range(experts):
+            line = jnp.sum(picked[e * cap : (e + 1) * cap] * eye, 0, keepdims=True)
+            p_send[group, e] = jnp.broadcast_to(line, (8, LANES))
+
+    sends_b = exchange(lambda group, expert: b_send.at[group, expert], b_slots, 2)
+    sends_p = exchange(lambda group, expert: p_send.at[group, expert], p_slots, 3)
+
+    def give_back(wanted):
+        for (dx, d), p_copy, b_copy in list(zip(offsets, sends_p, sends_b))[::-1]:
+            if dx in wanted:
+                p_copy.start()
+                b_copy.start()
 
     if structured:
 
-        def relay(k):
-            owner = column(k) * 4 + low
-
-            @pl.when((k > 0) & (k < 4))
-            def _():
-                landed(owner)
-
-                @pl.when(middle)
-                def _():
-                    push(owner, 0, k, at(me, jnp.where(k == 1, far, near))).start()
-
-                push(owner, 2, k, at(me, other_c)).start()
-
-        relay(1)
-        relay(2)
-
         @pl.when(middle)
         def _():
             relay(3)
+
+        @pl.when(jnp.logical_not(middle))
+        def _():
+            relay(2)
 
         arrivals(g_slots, 0)
         arrivals(u_slots, 1)
 
         def step(k, carry):
             start = column(k) * 4 + x * 2
-
-            @pl.when((k == 2) & jnp.logical_not(middle))
-            def _():
-                relay(3)
-
-            landed(start + 1 - place % 2)
-            work(start)
+            landed(start + 1 - place % 2, 0)
+            first_half(start)
+            landed(start + 1 - place % 2, 1)
+            second_half(start)
             return carry
 
-        lax.fori_loop(0, 4, step, 0)
+        lax.fori_loop(0, 3, step, 0)
+
+        @pl.when(jnp.logical_not(middle))
+        def _():
+            relay(3)
+
+        start = column(3) * 4 + x * 2
+        landed(start + 1 - place % 2, 0)
+        first_half(start)
+        landed(start + 1 - place % 2, 1)
     else:
 
         def settle(d, carry):
-            landed((place + d) % n)
+            for j in range(2):
+                landed((place + d) % n, j)
             return carry
 
         lax.fori_loop(1, n, settle, 0)
@@ -342,17 +401,18 @@
         arrivals(u_slots, 1)
 
         def step(j, carry):
-            work(j * per)
+            first_half(j * per)
+            second_half(j * per)
             return carry
 
-        lax.fori_loop(0, n // per, step, 0)
-
-    b_send[...] = inner_acc[...].astype(bf16).reshape(groups, experts, cap, width)
-    p_send[...] = jnp.broadcast_to(pick_acc[...], (groups * rows, LANES)).reshape(groups, experts, cap, LANES)
-    sends_b = exchange(lambda group, expert: b_send.at[group, expert], b_slots, 2)
-    sends_p = exchange(lambda group, expert: p_send.at[group, expert], p_slots, 3)
-    for copy in sends_p + sends_b:
-        copy.start()
+        lax.fori_loop(0, n // per - 1, step, 0)
+        start = n - per
+        first_half(start)
+
+    for dx in range(groups)[::-1]:
+        last_half(start, here + dx * (1 - 2 * here))
+        give_back((dx,))
+
     b_slots[here, me] = b_send[here, me]
     p_slots[here, me] = p_send[here, me]
     arrivals(p_slots, 3)
@@ -360,27 +420,41 @@
 
     normed = normed_s[...]
     part_inner = dot(disp, b_slots[0].reshape(rows, width), ((1,), (0,)))
-    picks = p_slots[0].reshape(rows, LANES)
     for group in range(1, groups):
         part_inner = part_inner + dot(disp, b_slots[group].reshape(rows, width), ((1,), (0,)))
-        picks = picks + p_slots[group].reshape(rows, LANES)
-    grad_pick = dot(disp.astype(f32), picks, ((1,), (0,)), lax.Precision.HIGHEST)[:, :1]
+    picks = jnp.zeros((tok, LANES), f32)
+    for e in range(experts):
+        line = p_slots[0, e, :1, :]
+        for group in range(1, groups):
+            line = line + p_slots[group, e, :1, :]
+        picks = jnp.where(route == e, line, picks)
+    grad_pick = jnp.sum(jnp.where(rank == lane, picks, 0.0), -1, keepdims=True)
     grad_logits = (grad_pick * pick) * (chosen - chance)
     grad_inner = pick * part_inner
+
+    def pack(at_row, line):
+        for c in range(pairs):
+            where = at_row * pairs + c
+            red_send[0, where : where + 1, :] = line[:, c * LANES : (c + 1) * LANES]
+
     inner_f = (normed * gain[...]).astype(bf16).astype(f32)
     for e in range(experts):
         column_e = grad_logits[:, e : e + 1]
         grad_inner = grad_inner + column_e * router_f[e : e + 1, :]
-        red_send[0, e : e + 1, :] = jnp.sum(inner_f * column_e, 0, keepdims=True)
-    red_send[0, experts : experts + 1, :] = jnp.sum(grad_inner * normed, 0, keepdims=True)
-    filler = red_send.shape[1] - experts - 1
-    if filler:
-        red_send[0, experts + 1 :, :] = jnp.zeros((filler, width), f32)
+        pack(e, jnp.sum(inner_f * column_e, 0, keepdims=True))
+    pack(experts, jnp.sum(grad_inner * normed, 0, keepdims=True))
     grad_normed = grad_inner * gain[...]
     grad_mid = rms * (
         grad_normed - normed * jnp.mean(grad_normed * normed, -1, keepdims=True)
     ) + grad_out[...].astype(f32)
     grad_acts[...] = grad_mid.astype(bf16)
+    results = [
+        pltpu.make_async_copy(source, target, out_sem.at[i])
+        for i, (source, target) in enumerate(
+            ((grad_acts, grad_acts_h), (grad_q, grad_q_h), (grad_k, grad_k_h), (grad_v, grad_v_h))
+        )
+    ]
+    results[0].start()
 
     reduces = [
         [
@@ -445,7 +519,7 @@
         return carry
 
     lax.fori_loop(0, pairs, backward, 0)
-    reduce_step(len(reduces) - 1)
+    results[1].start()
 
     def finish(i, carry):
         cols = pl.ds(pl.multiple_of(i * LANES, LANES), LANES)
@@ -467,6 +541,9 @@
         return carry
 
     lax.fori_loop(0, pairs, finish, 0)
+    results[2].start()
+    results[3].start()
+    reduce_step(len(reduces) - 1)
 
     @pl.when(place < n - 1)
     def _():
@@ -494,28 +571,35 @@
 
     lax.fori_loop(0, pairs, drain, 0)
     if structured:
-        push(place, 0, 0, at(me, near)).wait_send()
+        for j in range(2):
+            push(place, j, 0, 0, at(me, near), mine[j]).wait_send()
 
         @pl.when(middle)
         def _():
-            push(place, 1, 0, at(me, far)).wait_send()
+            for j in range(2):
+                push(place, j, 1, 0, at(me, far), mine[j]).wait_send()
 
         def sent(k, carry):
-            @pl.when((k > 0) & middle)
-            def _():
-                push(place, 0, k, at(me, near)).wait_send()
-
-            push(place, 2, k, at(me, near)).wait_send()
+            for j in range(2):
+
+                @pl.when((k > 0) & middle)
+                def _():
+                    push(place, j, 0, k, at(me, near)).wait_send()
+
+                push(place, j, 2, k, at(me, near)).wait_send()
             return carry
 
         lax.fori_loop(0, 4, sent, 0)
     else:
 
         def sent(d, carry):
-            push(place, 0, d, at(me, (place + d) % n)).wait_send()
+            for j in range(2):
+                push(place, j, 0, d, at(me, (place + d) % n), mine[j]).wait_send()
             return carry
 
         lax.fori_loop(1, n, sent, 0)
+    for copy in results:
+        copy.wait()
 
 
 def shards(acts, queries, keys, values, grad_out, gain, router, w_in, w_out, routes, tissue):
@@ -528,21 +612,25 @@
     frows = w_in.shape[1]
     span = tok + 2 * REACH
     pairs = width // LANES
-    lines = -(-(experts + 1) // 8) * 8
+    lines = (experts + 1) * pairs
+    per = max(1, 256 // frows)
     rounds = reduce_rounds(n, experts)
     most = max(len(masks) for masks in rounds)
     groups = 2 if n == 16 else 1
     bf16, f32 = jnp.bfloat16, jnp.float32
     vmem = pl.BlockSpec(memory_space=pltpu.VMEM)
+    hbm = pl.BlockSpec(memory_space=pl.ANY)
     big = jax.ShapeDtypeStruct((tok, width), bf16)
     dma = pltpu.SemaphoreType.DMA
     steps = 4 if n == 16 else n
     outs = pl.pallas_call(
         functools.partial(kernel, n, experts, cap, tissue.shape[1], groups),
-        out_shape=[big, big, big, big, jax.ShapeDtypeStruct((lines, width), f32)],
-        in_specs=[vmem] * 10 + [pl.BlockSpec(memory_space=pltpu.SMEM)],
-        out_specs=[vmem] * 5,
-        scratch_shapes=[
+        out_shape=[big, big, big, big, jax.ShapeDtypeStruct((lines, LANES), f32)],
+        in_specs=[hbm] * 5 + [vmem] * 2 + [hbm] * 2 + [vmem, pl.BlockSpec(memory_space=pltpu.SMEM)],
+        out_specs=[hbm] * 4 + [vmem],
+        scratch_shapes=[pltpu.VMEM((tok, width), bf16)] * 7
+        + [pltpu.VMEM((groups, rows, per * frows), f32)] * 2
+        + [
             pltpu.VMEM((n, 2, frows, width), bf16),
             pltpu.VMEM((span, width), bf16),
             pltpu.VMEM((span, width), bf16),
@@ -554,24 +642,25 @@
             pltpu.VMEM((groups, experts, cap, width), bf16),
             pltpu.VMEM((experts, cap, width), bf16),
             pltpu.VMEM((groups, experts, cap, width), bf16),
-            pltpu.VMEM((groups * rows, width), f32),
-            pltpu.VMEM((groups * rows, 1), f32),
+            pltpu.VMEM((groups, rows, width), f32),
+            pltpu.VMEM((groups, rows, 1), f32),
             pltpu.VMEM((groups, experts, cap, width), bf16),
             pltpu.VMEM((groups, experts, cap, width), bf16),
-            pltpu.VMEM((groups, experts, cap, LANES), f32),
-            pltpu.VMEM((groups, experts, cap, LANES), f32),
+            pltpu.VMEM((groups, experts, 8, LANES), f32),
+            pltpu.VMEM((groups, experts, 8, LANES), f32),
             pltpu.VMEM((2, tok, width), f32),
             pltpu.VMEM((pairs, 2, REACH, LANES), bf16),
             pltpu.VMEM((pairs, 2, REACH, LANES), bf16),
             pltpu.VMEM((pairs, 2, REACH, LANES), bf16),
             pltpu.VMEM((pairs, 2, REACH, LANES), bf16),
-            pltpu.VMEM((len(rounds), lines, width), f32),
-            pltpu.VMEM((len(rounds), most, lines, width), f32),
+            pltpu.VMEM((len(rounds), lines, LANES), f32),
+            pltpu.VMEM((len(rounds), most, lines, LANES), f32),
+            dma((7,)),
             dma((4,)),
             dma((2, 2)),
             dma((2, 2)),
-            dma((3, steps)),
-            dma((n,)),
+            dma((3, steps, 2)),
+            dma((n, 2)),
             dma((4, groups * experts)),
             dma((4, groups * experts)),
             dma((2, pairs)),
@@ -601,9 +690,13 @@
 def hand_out(*refs):
     for source, target in zip(refs[:4], refs[5:9]):
         target[...] = source[...]
-    experts = refs[9].shape[0]
-    refs[9][...] = refs[4][:experts, :]
-    refs[10][...] = refs[4][experts : experts + 1, :]
+    small, experts = refs[4], refs[9].shape[0]
+    pairs = small.shape[0] // (experts + 1)
+    for row in range(experts + 1):
+        target, line = (refs[9], row) if row < experts else (refs[10], 0)
+        for c in range(pairs):
+            where = row * pairs + c
+            target[line : line + 1, c * LANES : (c + 1) * LANES] = small[where : where + 1, :]
 
 
 def solution(mesh):

time: 86 us -> 78.4 us (0.912)
  Pallas kernels: 85 us -> 77.6 us
    pallas_call x1, Pallas kernels: 82.8 us -> 75.4 us  [shards(): pl.pallas_call(functools.partial(kernel, n, experts, cap, tissue.shape[1]...]
where the time goes in v1:
time: 78.4 us; the launch traced here: 78.2 us
  Pallas kernels  77.6 us (99%)
    pallas_call x1, Pallas kernels, shards(): pl.pallas_call(functools.partial(kernel, n, experts, cap, tissue.shape[1]...  75.4 us
    pallas_call x1, Pallas kernels, shards(): pl.pallas_call(hand_out, out_shape=[big, big, big, big, jax.ShapeDtypeStr...  2.18 us

profile of v1, /device:TPU:1, one launch (start us, length us, event | category | flops | bytes accessed | tf_op | source)
XLA Modules:
  0.0 78.2 jit_solution(18340630094523792579)
XLA Ops:
  0.6 75.4 %shard_map.154 = (bf16[128,1024]{1,0:T(8,128)(2,1)}, bf16[128,1024]{1,0:T(8,128)(2,1)}, bf16[128,1024]{1,0:T(8,128)(2,1)}, bf16[128,1024]{1,0:T(8,128)(2,1)}, f32[24,128]{1,0:T(8,128)}) custom-call(bf16[128,1024]{1,0:T(8,128)(2,1)} %bitcast.16, bf16[128,1024]{1,0:T(8,128)(2,1)} %bitcast.17, bf16[128,1024]{1,0:T(8,128)(2,1)} %bitcast.18, ...), custom_call_target="tpu_custom_call" | custom-call | tf_op jit(solution)/shard_map/pallas_call | solution.py:626
  76.0 2.2 %shard_map.155 = (bf16[128,1024]{1,0:T(8,128)(2,1)}, bf16[128,1024]{1,0:T(8,128)(2,1)}, bf16[128,1024]{1,0:T(8,128)(2,1)}, bf16[128,1024]{1,0:T(8,128)(2,1)}, f32[2,1024]{1,0:T(2,128)}, /*index=5*/f32[1,1024]{1,0:T(1,128)}) custom-call(bf16[128,1024]{1,0:T(8,128)(2,1)} %get-tuple-element.17.refs_0_, bf16[128,1024]{1,0:T(8,128)(2,1)} %get-tuple-element.18.refs_1_, ...), custom_call_target="tpu_custom_call" | custom-call | tf_op jit(solution)/shard_map/pallas_call | solution.py:678

commit v2 on v1

--- a/solution.py
+++ b/solution.py
@@ -52,8 +52,8 @@
     acts, queries, grad_out, grad_acts, grad_q, grad_k, grad_v, act_s, slope_s,
     weights, kx, vx, bias, probs, attn, normed_s, u_send, u_slots, g_send, g_slots,
     inner_acc, pick_acc, b_send, b_slots, p_send, p_slots, own_kv,
-    low_send, high_send, low_recv, high_recv, red_send, red_recv,
-    local_sem, out_sem, halo_ss, halo_rs, w_ss, w_rs, ex_ss, ex_rs, rim_ss, rim_rs, red_ss, red_rs,
+    stats, stat_send, stat_recv, side_bias, side_q, side_o, side_probs, red_send, red_recv,
+    local_sem, out_sem, halo_ss, halo_rs, w_ss, w_rs, ex_ss, ex_rs, nb_ss, nb_rs, red_ss, red_rs,
 ):
     tok, width = acts_h.shape
     span = tok + 2 * REACH
@@ -117,6 +117,9 @@
     near_by = jnp.abs(q_at - k_at) <= REACH
     allow = near_by & (k_at >= 0) & (k_at < n * tok) & ((live == 1) | (q_at == k_at))
     bias[...] = jnp.where(allow, 0.0, NEG).astype(f32)
+    live_own = live[:, REACH : REACH + tok] == 1
+    for r, near_side in enumerate(((col_at <= row_at) & (place > 0), (row_at <= col_at) & (place < n - 1))):
+        side_bias[r] = jnp.where(near_side & live_own, 0.0, NEG).astype(f32)
     own_copies[4].wait()
     moved_g = dot(disp, grad_out[...], ((0,), (0,))).astype(bf16)
     g_send[...] = moved_g.reshape(experts, cap, width)
@@ -132,6 +135,44 @@
         remote(src, dst.at[pl.ds(REACH + tok, REACH)], halo_ss.at[i, 1], halo_rs.at[i, 1], down)
         for i, (src, dst) in enumerate(((keys, kx), (values, vx)))
     ]
+
+    heads = 2 * pairs
+    targets = (up, down)
+    has = (place < n - 1, place > 0)
+    comes = (place > 0, place < n - 1)
+
+    def half_rows(t):
+        return pl.ds(t * pairs, pairs)
+
+    def half_cols(t):
+        return pl.ds(t * (width // 2), width // 2)
+
+    def beside_copy(kind, way):
+        if kind == 0:
+            src, dst = queries_h, side_q.at[way]
+        elif kind == 1:
+            src, dst = stat_send.at[0], stat_recv.at[way, 0]
+        elif kind < 4:
+            src, dst = (stat_send.at[1, half_rows(kind - 2)], stat_recv.at[way, 1, half_rows(kind - 2)])
+        else:
+            src, dst = grad_acts.at[:, half_cols(kind - 4)], side_o.at[way, :, half_cols(kind - 4)]
+        return remote(src, dst, nb_ss.at[kind, way], nb_rs.at[kind, way], targets[way])
+
+    def tell(kinds, ways=(0, 1)):
+        for way in ways:
+
+            @pl.when(has[way])
+            def _():
+                for kind in kinds:
+                    beside_copy(kind, way).start()
+
+    def hear(kinds):
+        for way in range(2):
+
+            @pl.when(comes[way])
+            def _():
+                for kind in kinds:
+                    beside_copy(kind, way).wait_recv()
 
     @pl.when(place < n - 1)
     def _():
@@ -230,6 +271,14 @@
         for copy in to_up:
             copy.wait_recv()
 
+    for way in range(2):
+
+        @pl.when(jnp.logical_not(comes[way]))
+        def _():
+            side_q[way] = jnp.zeros((tok, width), bf16)
+            side_o[way] = jnp.zeros((tok, width), bf16)
+            stat_recv[way] = jnp.zeros((2, heads, tok), f32)
+
     @pl.when(place == 0)
     def _():
         kx[pl.ds(0, REACH), :] = jnp.zeros((REACH, width), bf16)
@@ -268,20 +317,30 @@
         @pl.when(middle)
         def _():
             relay(2)
+
+    def keep(kind, i, line):
+        stats[kind] = jnp.where(
+            lane == 2 * i, line[:tok], jnp.where(lane == 2 * i + 1, line[tok:], stats[kind])
+        )
 
     def forward(i, carry):
         cols = pl.ds(pl.multiple_of(i * LANES, LANES), LANES)
         scores = dot(stack(queries[:, cols]), kx[:, cols], ((1,), (1,))) * HEAD ** (-0.5)
         both = jnp.concatenate([bias[...], bias[...]], 0)
         scores = scores + both
-        weight = jnp.exp(scores - jnp.max(scores, -1, keepdims=True))
-        prob = weight / jnp.sum(weight, -1, keepdims=True)
+        top = jnp.max(scores, -1, keepdims=True)
+        weight = jnp.exp(scores - top)
+        total = jnp.sum(weight, -1, keepdims=True)
+        prob = weight / total
         probs[i] = prob
+        keep(0, i, top + jnp.log(total))
         mixed = dot(prob.astype(bf16), vx[:, cols], ((1,), (0,)))
         attn[:, cols] = jnp.where(half, mixed[:tok], mixed[tok:])
         return carry
 
+    stats[...] = jnp.zeros_like(stats)
     lax.fori_loop(0, pairs, forward, 0)
+    stat_send[0] = jnp.transpose(stats[0])[:heads]
 
     own_copies[6].wait()
     mid = acts[...].astype(f32) + attn[...]
@@ -294,6 +353,14 @@
     sends_u = exchange(lambda group, expert: u_send.at[expert], u_slots, 1)
     for copy in sends_u:
         copy.start()
+    late = (place == n - 5, place == 4) if structured else (False, False)
+    tell((1,))
+    for way in range(2):
+
+        @pl.when(has[way] & jnp.logical_not(late[way]))
+        def _():
+            beside_copy(0, way).start()
+
 
     inner_f = inner.astype(f32)
     router_f = router[...].astype(f32)
@@ -412,6 +479,31 @@
     for dx in range(groups)[::-1]:
         last_half(start, here + dx * (1 - 2 * here))
         give_back((dx,))
+
+    hear((0, 1))
+
+    def column_of(table, at_lane):
+        return jnp.sum(jnp.where(lane == at_lane, table, 0.0), -1, keepdims=True)
+
+    def upright(table):
+        if table.shape[0] < tok:
+            table = jnp.concatenate([table, jnp.zeros((tok - table.shape[0], tok), f32)], 0)
+        return jnp.transpose(table)
+
+    for way in range(2):
+        stats[2 + way] = upright(stat_recv[way, 0])
+    own = pl.ds(REACH, tok)
+
+    def beside_probs(i, carry):
+        cols = pl.ds(pl.multiple_of(i * LANES, LANES), LANES)
+        for way in range(2):
+            scores = dot(stack(side_q[way, :, cols]), kx[own, cols], ((1,), (1,))) * HEAD ** (-0.5)
+            scores = scores + jnp.concatenate([side_bias[way], side_bias[way]], 0)
+            line = jnp.concatenate([column_of(stats[2 + way], 2 * i), column_of(stats[2 + way], 2 * i + 1)], 0)
+            side_probs[i, way * 2 * tok : (way + 1) * 2 * tok, :] = jnp.exp(scores - line)
+        return carry
+
+    lax.fori_loop(0, pairs, beside_probs, 0)
 
     b_slots[here, me] = b_send[here, me]
     p_slots[here, me] = p_send[here, me]
@@ -455,6 +547,13 @@
         )
     ]
     results[0].start()
+    for way in range(2):
+
+        @pl.when(has[way] & late[way])
+        def _():
+            beside_copy(0, way).start()
+
+    tell((4,))
 
     reduces = [
         [
@@ -479,16 +578,10 @@
     for copy in reduces[0]:
         copy.start()
 
-    def rim_down(i):
-        return remote(low_send.at[i], low_recv.at[i], rim_ss.at[0, i], rim_rs.at[0, i], down)
-
-    def rim_up(i):
-        return remote(high_send.at[i], high_recv.at[i], rim_ss.at[1, i], rim_rs.at[1, i], up)
-
     def backward(i, carry):
         for j in range(len(reduces) - 1):
 
-            @pl.when(i == 4 + j)
+            @pl.when(i == pairs // 2 + j)
             def _():
                 reduce_step(j)
 
@@ -497,50 +590,42 @@
         q_stack = stack(queries[:, cols])
         prob = probs[i]
         grad_probs = dot(o_stack, vx[:, cols], ((1,), (1,)))
-        value_terms = dot(prob.astype(bf16), o_stack, ((0,), (0,)))
+        own_value = dot(prob[:, REACH : REACH + tok].astype(bf16), o_stack, ((0,), (0,)))
         delta = jnp.sum(prob * grad_probs, -1, keepdims=True)
+        keep(1, i, delta)
         grad_scores = (prob * (grad_probs - delta) * HEAD ** (-0.5)).astype(bf16)
         query_terms = dot(grad_scores, kx[:, cols], ((1,), (0,)))
         grad_q[:, cols] = jnp.where(half, query_terms[:tok], query_terms[tok:]).astype(bf16)
-        key_terms = dot(grad_scores, q_stack, ((0,), (0,)))
-        for slot_at, terms in enumerate((key_terms, value_terms)):
-            low_send[i, slot_at] = terms[:REACH].astype(bf16)
-            own_kv[slot_at, :, cols] = terms[REACH : REACH + tok]
-            high_send[i, slot_at] = terms[REACH + tok :].astype(bf16)
-
-        @pl.when(place > 0)
-        def _():
-            rim_down(i).start()
-
-        @pl.when(place < n - 1)
-        def _():
-            rim_up(i).start()
-
+        own_key = dot(grad_scores[:, REACH : REACH + tok], q_stack, ((0,), (0,)))
+        own_kv[0, :, cols] = own_key
+        own_kv[1, :, cols] = own_value
         return carry
 
-    lax.fori_loop(0, pairs, backward, 0)
+    for t in range(2):
+        lax.fori_loop(t * (pairs // 2), (t + 1) * (pairs // 2), backward, 0)
+        stat_send[1, half_rows(t)] = jnp.transpose(stats[1])[t * pairs : (t + 1) * pairs]
+        tell((2, 5) if t == 0 else (3,))
     results[1].start()
 
-    def finish(i, carry):
+    def finish(t, i, carry):
         cols = pl.ds(pl.multiple_of(i * LANES, LANES), LANES)
-
-        @pl.when(place > 0)
-        def _():
-            rim_up(i).wait_recv()
-            for slot_at in range(2):
-                own_kv[slot_at, :REACH, cols] += high_recv[i, slot_at].astype(f32)
-
-        @pl.when(place < n - 1)
-        def _():
-            rim_down(i).wait_recv()
-            for slot_at in range(2):
-                own_kv[slot_at, tok - REACH :, cols] += low_recv[i, slot_at].astype(f32)
-
-        grad_k[:, cols] = own_kv[0, :, cols].astype(bf16)
-        grad_v[:, cols] = own_kv[1, :, cols].astype(bf16)
+        o_all = jnp.concatenate([stack(side_o[way, :, cols]) for way in range(2)], 0)
+        q_all = jnp.concatenate([stack(side_q[way, :, cols]) for way in range(2)], 0)
+        prob = side_probs[i]
+        line = jnp.concatenate(
+            [column_of(stats[2 + way], 2 * i + h - t * pairs) for way in range(2) for h in range(2)], 0
+        )
+        grad_probs = dot(o_all, vx[own, cols], ((1,), (1,)))
+        grad_scores = (prob * (grad_probs - line) * HEAD ** (-0.5)).astype(bf16)
+        grad_k[:, cols] = (own_kv[0, :, cols] + dot(grad_scores, q_all, ((0,), (0,)))).astype(bf16)
+        grad_v[:, cols] = (own_kv[1, :, cols] + dot(prob.astype(bf16), o_all, ((0,), (0,)))).astype(bf16)
         return carry
 
-    lax.fori_loop(0, pairs, finish, 0)
+    for t in range(2):
+        hear((2 + t, 4 + t))
+        for way in range(2):
+            stats[2 + way] = upright(stat_recv[way, 1, t * pairs : (t + 1) * pairs])
+        lax.fori_loop(t * (pairs // 2), (t + 1) * (pairs // 2), functools.partial(finish, t), 0)
     results[2].start()
     results[3].start()
     reduce_step(len(reduces) - 1)
@@ -558,18 +643,13 @@
     for copy in sends_g + sends_u + sends_b + sends_p + [c for group in reduces for c in group]:
         copy.wait_send()
 
-    def drain(i, carry):
-        @pl.when(place > 0)
-        def _():
-            rim_down(i).wait_send()
-
-        @pl.when(place < n - 1)
-        def _():
-            rim_up(i).wait_send()
-
-        return carry
-
-    lax.fori_loop(0, pairs, drain, 0)
+    for way in range(2):
+
+        @pl.when(has[way])
+        def _():
+            for kind in range(6):
+                beside_copy(kind, way).wait_send()
+
     if structured:
         for j in range(2):
             push(place, j, 0, 0, at(me, near), mine[j]).wait_send()
@@ -649,10 +729,13 @@
             pltpu.VMEM((groups, experts, 8, LANES), f32),
             pltpu.VMEM((groups, experts, 8, LANES), f32),
             pltpu.VMEM((2, tok, width), f32),
-            pltpu.VMEM((pairs, 2, REACH, LANES), bf16),
-            pltpu.VMEM((pairs, 2, REACH, LANES), bf16),
-            pltpu.VMEM((pairs, 2, REACH, LANES), bf16),
-            pltpu.VMEM((pairs, 2, REACH, LANES), bf16),
+            pltpu.VMEM((4, tok, LANES), f32),
+            pltpu.VMEM((2, 2 * pairs, tok), f32),
+            pltpu.VMEM((2, 2, 2 * pairs, tok), f32),
+            pltpu.VMEM((2, tok, tok), f32),
+            pltpu.VMEM((2, tok, width), bf16),
+            pltpu.VMEM((2, tok, width), bf16),
+            pltpu.VMEM((pairs, 4 * tok, tok), f32),
             pltpu.VMEM((len(rounds), lines, LANES), f32),
             pltpu.VMEM((len(rounds), most, lines, LANES), f32),
             dma((7,)),
@@ -663,8 +746,8 @@
             dma((n, 2)),
             dma((4, groups * experts)),
             dma((4, groups * experts)),
-            dma((2, pairs)),
-            dma((2, pairs)),
+            dma((6, 2)),
+            dma((6, 2)),
             dma((len(rounds), most)),
             dma((len(rounds), most)),
         ],

time: 78.4 us -> 80.1 us (1.022)
  Pallas kernels: 77.6 us -> 78.8 us
    pallas_call x1, Pallas kernels: 75.4 us -> 76.7 us  [shards(): pl.pallas_call(functools.partial(kernel, n, experts, cap, tissue.shape[1]...]
where the time goes in v2:
time: 80.1 us; the launch traced here: 79.5 us
  Pallas kernels  78.8 us (98%)
    pallas_call x1, Pallas kernels, shards(): pl.pallas_call(functools.partial(kernel, n, experts, cap, tissue.shape[1]...  76.7 us
    pallas_call x1, Pallas kernels, shards(): pl.pallas_call(hand_out, out_shape=[big, big, big, big, jax.ShapeDtypeStr...  2.18 us

profile of v2, /device:TPU:1, one launch (start us, length us, event | category | flops | bytes accessed | tf_op | source)
XLA Modules:
  0.0 79.5 jit_solution(5435635681584179091)
XLA Ops:
  0.6 76.7 %shard_map.154 = (bf16[128,1024]{1,0:T(8,128)(2,1)}, bf16[128,1024]{1,0:T(8,128)(2,1)}, bf16[128,1024]{1,0:T(8,128)(2,1)}, bf16[128,1024]{1,0:T(8,128)(2,1)}, f32[24,128]{1,0:T(8,128)}) custom-call(bf16[128,1024]{1,0:T(8,128)(2,1)} %bitcast.16, bf16[128,1024]{1,0:T(8,128)(2,1)} %bitcast.17, bf16[128,1024]{1,0:T(8,128)(2,1)} %bitcast.18, ...), custom_call_target="tpu_custom_call" | custom-call | tf_op jit(solution)/shard_map/pallas_call | solution.py:706
  77.3 2.2 %shard_map.155 = (bf16[128,1024]{1,0:T(8,128)(2,1)}, bf16[128,1024]{1,0:T(8,128)(2,1)}, bf16[128,1024]{1,0:T(8,128)(2,1)}, bf16[128,1024]{1,0:T(8,128)(2,1)}, f32[2,1024]{1,0:T(2,128)}, /*index=5*/f32[1,1024]{1,0:T(1,128)}) custom-call(bf16[128,1024]{1,0:T(8,128)(2,1)} %get-tuple-element.17.refs_0_, bf16[128,1024]{1,0:T(8,128)(2,1)} %get-tuple-element.18.refs_1_, ...), custom_call_target="tpu_custom_call" | custom-call | tf_op jit(solution)/shard_map/pallas_call | solution.py:761

commit v3 on v2

--- a/solution.py
+++ b/solution.py
@@ -52,8 +52,8 @@
     acts, queries, grad_out, grad_acts, grad_q, grad_k, grad_v, act_s, slope_s,
     weights, kx, vx, bias, probs, attn, normed_s, u_send, u_slots, g_send, g_slots,
     inner_acc, pick_acc, b_send, b_slots, p_send, p_slots, own_kv,
-    stats, stat_send, stat_recv, side_bias, side_q, side_o, side_probs, red_send, red_recv,
-    local_sem, out_sem, halo_ss, halo_rs, w_ss, w_rs, ex_ss, ex_rs, nb_ss, nb_rs, red_ss, red_rs,
+    stats, stat_send, stat_recv, side_bias, side_q, side_o, side_probs, relay_v, red_send, red_recv,
+    local_sem, out_sem, halo_ss, halo_rs, w_ss, w_rs, ex_ss, ex_rs, nb_ss, nb_rs, relay_sem, red_ss, red_rs,
 ):
     tok, width = acts_h.shape
     span = tok + 2 * REACH
@@ -78,7 +78,7 @@
     peers = [at(flip(me, e), flip(place, m)) for masks in rounds for e, m in masks]
     if structured:
         z = place // 4
-        peers += [at(me, (place + 1) % n), at(me, (place + n - 1) % n)]
+        peers += [at(me, (place + d) % n) for d in (1, n - 1, 3, n - 3)]
     else:
         peers += [at(me, (place + d) % n) for d in range(1, n)]
         peers += [at((me + d) % experts, place) for d in range(1, experts)]
@@ -174,15 +174,38 @@
                 for kind in kinds:
                     beside_copy(kind, way).wait_recv()
 
-    @pl.when(place < n - 1)
-    def _():
-        for copy in to_up:
-            copy.start()
-
-    @pl.when(place > 0)
-    def _():
-        for copy in to_down:
-            copy.start()
+    if structured:
+        seat = place % 4
+        over = (
+            remote(values, relay_v, halo_ss.at[1, 0], relay_sem.at[0], at(me, (place + n - 2) % n)),
+            remote(values, relay_v, halo_ss.at[1, 1], relay_sem.at[0], at(me, (place + 2) % n)),
+        )
+        onward = (
+            remote(relay_v, vx.at[pl.ds(0, REACH)], relay_sem.at[1], halo_rs.at[1, 0], at(me, (place + 3) % n)),
+            remote(
+                relay_v, vx.at[pl.ds(REACH + tok, REACH)], relay_sem.at[1], halo_rs.at[1, 1], at(me, (place + n - 3) % n)
+            ),
+        )
+        turns = ((seat == 1) & (place < n - 3), (seat == 2) & (place > 2))
+        aside = (seat == 3, seat == 0)
+    else:
+        aside = (False, False)
+
+    for way, copies in enumerate((to_up, to_down)):
+
+        @pl.when(has[way])
+        def _():
+            copies[0].start()
+
+        @pl.when(has[way] & jnp.logical_not(aside[way]))
+        def _():
+            copies[1].start()
+
+        if structured:
+
+            @pl.when(has[way] & aside[way])
+            def _():
+                over[way].start()
 
     def push(owner, j, kind, step, where, src=None):
         return remote(
@@ -265,6 +288,13 @@
 
     own_copies[2].wait()
     own_copies[3].wait()
+    if structured:
+        for way in range(2):
+
+            @pl.when(turns[way])
+            def _():
+                over[way].wait_recv()
+                onward[way].start()
 
     @pl.when(place > 0)
     def _():
@@ -479,6 +509,12 @@
     for dx in range(groups)[::-1]:
         last_half(start, here + dx * (1 - 2 * here))
         give_back((dx,))
+
+    for way in range(2):
+
+        @pl.when(has[way] & late[way])
+        def _():
+            beside_copy(0, way).start()
 
     hear((0, 1))
 
@@ -547,12 +583,6 @@
         )
     ]
     results[0].start()
-    for way in range(2):
-
-        @pl.when(has[way] & late[way])
-        def _():
-            beside_copy(0, way).start()
-
     tell((4,))
 
     reduces = [
@@ -639,6 +669,13 @@
     def _():
         for copy in to_down:
             copy.wait_send()
+
+    if structured:
+        for way in range(2):
+
+            @pl.when(turns[way])
+            def _():
+                onward[way].wait_send()
 
     for copy in sends_g + sends_u + sends_b + sends_p + [c for group in reduces for c in group]:
         copy.wait_send()
@@ -736,6 +773,7 @@
             pltpu.VMEM((2, tok, width), bf16),
             pltpu.VMEM((2, tok, width), bf16),
             pltpu.VMEM((pairs, 4 * tok, tok), f32),
+            pltpu.VMEM((tok, width), bf16),
             pltpu.VMEM((len(rounds), lines, LANES), f32),
             pltpu.VMEM((len(rounds), most, lines, LANES), f32),
             dma((7,)),
@@ -748,6 +786,7 @@
             dma((4, groups * experts)),
             dma((6, 2)),
             dma((6, 2)),
+            dma((2,)),
             dma((len(rounds), most)),
             dma((len(rounds), most)),
         ],

time: 80.1 us -> 76 us (0.949)
  Pallas kernels: 78.8 us -> 75 us
    pallas_call x1, Pallas kernels: 76.7 us -> 72.8 us  [shards(): pl.pallas_call(functools.partial(kernel, n, experts, cap, tissue.shape[1]...]
where the time goes in v3:
time: 76 us; the launch traced here: 75.6 us
  Pallas kernels  75 us (99%)
    pallas_call x1, Pallas kernels, shards(): pl.pallas_call(functools.partial(kernel, n, experts, cap, tissue.shape[1]...  72.8 us
    pallas_call x1, Pallas kernels, shards(): pl.pallas_call(hand_out, out_shape=[big, big, big, big, jax.ShapeDtypeStr...  2.18 us

profile of v3, /device:TPU:1, one launch (start us, length us, event | category | flops | bytes accessed | tf_op | source)
XLA Modules:
  0.0 75.6 jit_solution(7057502481728055796)
XLA Ops:
  0.6 72.8 %shard_map.154 = (bf16[128,1024]{1,0:T(8,128)(2,1)}, bf16[128,1024]{1,0:T(8,128)(2,1)}, bf16[128,1024]{1,0:T(8,128)(2,1)}, bf16[128,1024]{1,0:T(8,128)(2,1)}, f32[24,128]{1,0:T(8,128)}) custom-call(bf16[128,1024]{1,0:T(8,128)(2,1)} %bitcast.16, bf16[128,1024]{1,0:T(8,128)(2,1)} %bitcast.17, bf16[128,1024]{1,0:T(8,128)(2,1)} %bitcast.18, ...), custom_call_target="tpu_custom_call" | custom-call | tf_op jit(solution)/shard_map/pallas_call | solution.py:743
  73.4 2.2 %shard_map.155 = (bf16[128,1024]{1,0:T(8,128)(2,1)}, bf16[128,1024]{1,0:T(8,128)(2,1)}, bf16[128,1024]{1,0:T(8,128)(2,1)}, bf16[128,1024]{1,0:T(8,128)(2,1)}, f32[2,1024]{1,0:T(2,128)}, /*index=5*/f32[1,1024]{1,0:T(1,128)}) custom-call(bf16[128,1024]{1,0:T(8,128)(2,1)} %get-tuple-element.17.refs_0_, bf16[128,1024]{1,0:T(8,128)(2,1)} %get-tuple-element.18.refs_1_, ...), custom_call_target="tpu_custom_call" | custom-call | tf_op jit(solution)/shard_map/pallas_call | solution.py:800

commit v4 on v3

--- a/solution.py
+++ b/solution.py
@@ -582,9 +582,6 @@
             ((grad_acts, grad_acts_h), (grad_q, grad_q_h), (grad_k, grad_k_h), (grad_v, grad_v_h))
         )
     ]
-    results[0].start()
-    tell((4,))
-
     reduces = [
         [
             remote(red_send.at[j], red_recv.at[j, i], red_ss.at[j, i], red_rs.at[j, i], at(flip(me, e), flip(place, m)))
@@ -592,6 +589,10 @@
         ]
         for j, masks in enumerate(rounds)
     ]
+    for copy in reduces[0]:
+        copy.start()
+    results[0].start()
+    tell((4,))
 
     def reduce_step(j):
         total = red_send[j]
@@ -605,16 +606,8 @@
         else:
             small_out[...] = total
 
-    for copy in reduces[0]:
-        copy.start()
 
     def backward(i, carry):
-        for j in range(len(reduces) - 1):
-
-            @pl.when(i == pairs // 2 + j)
-            def _():
-                reduce_step(j)
-
         cols = pl.ds(pl.multiple_of(i * LANES, LANES), LANES)
         o_stack = stack(grad_acts[:, cols])
         q_stack = stack(queries[:, cols])
@@ -636,6 +629,8 @@
         stat_send[1, half_rows(t)] = jnp.transpose(stats[1])[t * pairs : (t + 1) * pairs]
         tell((2, 5) if t == 0 else (3,))
     results[1].start()
+    for j in range(len(reduces) - 1):
+        reduce_step(j)
 
     def finish(t, i, carry):
         cols = pl.ds(pl.multiple_of(i * LANES, LANES), LANES)

time: 76 us -> 72.6 us (0.955)
  Pallas kernels: 75 us -> 71.3 us
    pallas_call x1, Pallas kernels: 72.8 us -> 69.2 us  [shards(): pl.pallas_call(functools.partial(kernel, n, experts, cap, tissue.shape[1]...]
where the time goes in v4:
time: 72.6 us; the launch traced here: 72 us
  Pallas kernels  71.3 us (98%)
    pallas_call x1, Pallas kernels, shards(): pl.pallas_call(functools.partial(kernel, n, experts, cap, tissue.shape[1]...  69.2 us
    pallas_call x1, Pallas kernels, shards(): pl.pallas_call(hand_out, out_shape=[big, big, big, big, jax.ShapeDtypeStr...  2.18 us

profile of v4, /device:TPU:1, one launch (start us, length us, event | category | flops | bytes accessed | tf_op | source)
XLA Modules:
  0.0 72.0 jit_solution(14717834547577429394)
XLA Ops:
  0.6 69.2 %shard_map.154 = (bf16[128,1024]{1,0:T(8,128)(2,1)}, bf16[128,1024]{1,0:T(8,128)(2,1)}, bf16[128,1024]{1,0:T(8,128)(2,1)}, bf16[128,1024]{1,0:T(8,128)(2,1)}, f32[24,128]{1,0:T(8,128)}) custom-call(bf16[128,1024]{1,0:T(8,128)(2,1)} %bitcast.16, bf16[128,1024]{1,0:T(8,128)(2,1)} %bitcast.17, bf16[128,1024]{1,0:T(8,128)(2,1)} %bitcast.18, ...), custom_call_target="tpu_custom_call" | custom-call | tf_op jit(solution)/shard_map/pallas_call | solution.py:738
  69.8 2.2 %shard_map.155 = (bf16[128,1024]{1,0:T(8,128)(2,1)}, bf16[128,1024]{1,0:T(8,128)(2,1)}, bf16[128,1024]{1,0:T(8,128)(2,1)}, bf16[128,1024]{1,0:T(8,128)(2,1)}, f32[2,1024]{1,0:T(2,128)}, /*index=5*/f32[1,1024]{1,0:T(1,128)}) custom-call(bf16[128,1024]{1,0:T(8,128)(2,1)} %get-tuple-element.17.refs_0_, bf16[128,1024]{1,0:T(8,128)(2,1)} %get-tuple-element.18.refs_1_, ...), custom_call_target="tpu_custom_call" | custom-call | tf_op jit(solution)/shard_map/pallas_call | solution.py:795
